TPU v7x, 512 devices: a whole 4x8x8 slice. The times are simulated.
512 devices in a mesh: phase: 16 (over z, core), rows: 32 (over y, x).
Axes of the slice: x: 4, y: 8, z: 8, core: 2. Of those that a mesh axis runs over, the one named last changes fastest.
Arguments:
- start: bfloat16 [16, 32768, 256], P('phase', 'rows')
- blocks: bfloat16 [16, 256, 4, 128, 128], P('phase', 'rows')
- cols: int32 [16, 256, 4], P('phase', 'rows'), may hold values from 0 to 255, as said below
- counts: int32 [16, 256], P('phase', 'rows'), may hold values from 1 to 4, as said below
Outputs:
- basis: float32 [16, 32768, 256], P('phase', 'rows')
- factor: float32 [16, 256, 256], P('phase')
Inputs may be any that keep to these rules, and one draw needn't show every extreme that they name: cols[q, i, 0] = i; the other slots of block row i name distinct block rows (i + o) mod 256 with 1 <= |o| <= 2. Block row i of section q uses its first counts[q, i] slots; every section has a block row that uses all 4.
All inputs are finite; a program needn't handle non-finite values.
Results may differ from a plain program's by a relative error of at most 0.012.
Values may be sent and summed in bfloat16 or wider, within the bound.
No kernel may reach another device: no remote copies, remote signals or barrier semaphores. Data moves between devices by JAX's collectives and lax.ppermute only.
A program may use at most 64 MiB of HBM per device.

v0:
```python
import jax
import jax.numpy as jnp
from jax import lax
from jax.sharding import PartitionSpec as P

HB = 2


def with_halo(array, sides, width):
    for axis, dim in sides:
        peers, length = (lax.axis_size(axis), array.shape[dim])
        up = [(i, (i + 1) % peers) for i in range(peers)]
        down = [(j, i) for i, j in up]
        last = lax.slice_in_dim(array, length - width, length, axis=dim)
        leading = lax.slice_in_dim(array, 0, width, axis=dim)
        before = lax.ppermute(last, axis, up)
        after = lax.ppermute(leading, axis, down)
        array = jnp.concatenate([before, array, after], axis=dim)
    return array


def passed_along(value, axis, steps):
    count = lax.axis_size(axis)
    pairs = [(source, (source + steps) % count) for source in range(count)]
    return lax.ppermute(value, axis, pairs)


def body(start, blocks, cols, counts):
    block_rows = blocks.shape[1]
    slot_count = blocks.shape[2]
    tile_size = blocks.shape[3]
    rows_here = start.shape[1]
    owners = lax.axis_size("rows")
    sections = lax.axis_size("phase")
    total_blocks = block_rows * owners
    first_block = lax.axis_index("rows") * block_rows
    local_index = jnp.mod(cols[0] - first_block + HB, total_blocks)
    live_slots = jnp.arange(slot_count, dtype=jnp.int32)[None, :] < counts[0][:, None]
    zero_value = jnp.zeros((), jnp.bfloat16)
    kept_blocks = jnp.where(live_slots[:, :, None, None], blocks[0], zero_value)
    rim_rows = HB * tile_size

    def advance(current):
        columns = current.shape[1]
        extended = with_halo(current, (("rows", 0),), rim_rows)
        row_tiles = extended.reshape(block_rows + 2 * HB, tile_size, columns)
        picked = row_tiles[local_index]
        product = jnp.einsum(
            "ijab,ijbk->iak", kept_blocks, picked, preferred_element_type=jnp.float32
        )
        return product.reshape(rows_here, columns).astype(jnp.bfloat16)

    def turn_one(turn_index, current):
        return passed_along(advance(current), "phase", 1)

    arrived = lax.fori_loop(0, sections, turn_one, start[0])
    gram_term = lax.dot_general(
        arrived, arrived, (((0,), (0,)), ((), ())), preferred_element_type=jnp.float32
    )
    gram_total = lax.psum(gram_term.astype(jnp.bfloat16), "rows").astype(jnp.float32) / (
        rows_here * owners
    )
    lower_factor = jnp.linalg.cholesky(gram_total)
    basis_out = jax.scipy.linalg.solve_triangular(
        lower_factor, arrived.astype(jnp.float32).T, lower=True
    ).T
    return (basis_out[None], lower_factor.T[None])


def solution(mesh):
    placed = (
        P("phase", "rows", None),
        P("phase", "rows", None, None, None),
        P("phase", "rows", None),
        P("phase", "rows"),
    )
    return jax.shard_map(
        body,
        mesh=mesh,
        in_specs=placed,
        out_specs=(P("phase", "rows", None), P("phase", None, None)),
        check_vma=False,
    )
```

profile of v0, /device:TPU:2, one launch (start us, length us, event | category | flops | bytes accessed | tf_op | source)
XLA Modules:
  0.0 634.1 jit_solution(17564700713426844968)
XLA Ops:
  10.4 398.1 %while.11 = (s32[]{:T(128)}, bf16[1024,256]{1,0:T(8,128)(2,1)S(1)}, s32[8,4]{0,1:T(4,128)S(1)}, bf16[8,4,128,128]{3,2,1,0:T(8,128)(2,1)}, s32[]{:T(128)}) while((s32[]{:T(128)}, bf16[1024,256]{1,0:T(8,128)(2,1)S(1)}, s32[8,4]{0,1:T(4,128)S(1)}, bf16[8,4,128,128]{3,2,1,0:T(8,128)(2,1)}, s32[]{:T(128)}) %tuple.54), condition=%wide.region_1.2_spmd, body=%wide.region_0.1_spmd.sunk | while | flops 271058016 | bytes 13112501 | solution.py:56
  10.4 7.8 %collective-permute-start = (bf16[256,256]{1,0:T(8,128)(2,1)S(1)}, bf16[256,256]{1,0:T(8,128)(2,1)S(1)}, u32[]{:S(2)}, u32[]{:S(2)}) collective-permute-start(bf16[256,256]{1,0:T(8,128)(2,1)S(1)} %get-tuple-element.117), channel_id=1, source_target_pairs={{1,0},{2,1},{3,2},{4,3},{5,4},{6,5},{7,6},{8,7},{9,8},{10,9},{11,1... | collective-permute-start | bytes 393224 | tf_op jit(solution)/shard_map/while/body/eval_jaxpr/ppermute | solution.py:17
  20.7 4.4 collective-permute-done.1
  27.6 13.0 %collective-permute-done.2 = bf16[1024,256]{1,0:T(8,128)(2,1)S(1)} collective-permute-done((bf16[1024,256]{1,0:T(8,128)(2,1)S(1)}, bf16[1024,256]{1,0:T(8,128)(2,1)S(1)}, u32[]{:S(2)}, u32[]{:S(2)}) %collective-permute-start.2) | collective-permute-done | bytes 524320 | tf_op jit(solution)/shard_map/while/body/eval_jaxpr/ppermute | solution.py:25
  40.6 6.4 %collective-permute-start = (bf16[256,256]{1,0:T(8,128)(2,1)S(1)}, bf16[256,256]{1,0:T(8,128)(2,1)S(1)}, u32[]{:S(2)}, u32[]{:S(2)}) collective-permute-start(bf16[256,256]{1,0:T(8,128)(2,1)S(1)} %get-tuple-element.117), channel_id=1, source_target_pairs={{1,0},{2,1},{3,2},{4,3},{5,4},{6,5},{7,6},{8,7},{9,8},{10,9},{11,1... | collective-permute-start | bytes 393224 | tf_op jit(solution)/shard_map/while/body/eval_jaxpr/ppermute | solution.py:17
  49.5 4.4 collective-permute-done.1
  56.4 9.8 %collective-permute-done.2 = bf16[1024,256]{1,0:T(8,128)(2,1)S(1)} collective-permute-done((bf16[1024,256]{1,0:T(8,128)(2,1)S(1)}, bf16[1024,256]{1,0:T(8,128)(2,1)S(1)}, u32[]{:S(2)}, u32[]{:S(2)}) %collective-permute-start.2) | collective-permute-done | bytes 524320 | tf_op jit(solution)/shard_map/while/body/eval_jaxpr/ppermute | solution.py:25
  66.2 5.2 collective-permute-start
  74.0 4.4 collective-permute-done.1
  80.9 9.8 %collective-permute-done.2 = bf16[1024,256]{1,0:T(8,128)(2,1)S(1)} collective-permute-done((bf16[1024,256]{1,0:T(8,128)(2,1)S(1)}, bf16[1024,256]{1,0:T(8,128)(2,1)S(1)}, u32[]{:S(2)}, u32[]{:S(2)}) %collective-permute-start.2) | collective-permute-done | bytes 524320 | tf_op jit(solution)/shard_map/while/body/eval_jaxpr/ppermute | solution.py:25
  90.7 5.2 collective-permute-start
  98.4 4.4 collective-permute-done.1
  105.3 9.8 %collective-permute-done.2 = bf16[1024,256]{1,0:T(8,128)(2,1)S(1)} collective-permute-done((bf16[1024,256]{1,0:T(8,128)(2,1)S(1)}, bf16[1024,256]{1,0:T(8,128)(2,1)S(1)}, u32[]{:S(2)}, u32[]{:S(2)}) %collective-permute-start.2) | collective-permute-done | bytes 524320 | tf_op jit(solution)/shard_map/while/body/eval_jaxpr/ppermute | solution.py:25
  115.1 5.2 collective-permute-start
  122.9 4.4 collective-permute-done.1
  129.8 9.8 %collective-permute-done.2 = bf16[1024,256]{1,0:T(8,128)(2,1)S(1)} collective-permute-done((bf16[1024,256]{1,0:T(8,128)(2,1)S(1)}, bf16[1024,256]{1,0:T(8,128)(2,1)S(1)}, u32[]{:S(2)}, u32[]{:S(2)}) %collective-permute-start.2) | collective-permute-done | bytes 524320 | tf_op jit(solution)/shard_map/while/body/eval_jaxpr/ppermute | solution.py:25
  139.6 5.2 collective-permute-start
  147.3 4.4 collective-permute-done.1
  154.2 9.8 %collective-permute-done.2 = bf16[1024,256]{1,0:T(8,128)(2,1)S(1)} collective-permute-done((bf16[1024,256]{1,0:T(8,128)(2,1)S(1)}, bf16[1024,256]{1,0:T(8,128)(2,1)S(1)}, u32[]{:S(2)}, u32[]{:S(2)}) %collective-permute-start.2) | collective-permute-done | bytes 524320 | tf_op jit(solution)/shard_map/while/body/eval_jaxpr/ppermute | solution.py:25
  164.0 5.2 collective-permute-start
  171.8 4.4 collective-permute-done.1
  178.7 9.8 %collective-permute-done.2 = bf16[1024,256]{1,0:T(8,128)(2,1)S(1)} collective-permute-done((bf16[1024,256]{1,0:T(8,128)(2,1)S(1)}, bf16[1024,256]{1,0:T(8,128)(2,1)S(1)}, u32[]{:S(2)}, u32[]{:S(2)}) %collective-permute-start.2) | collective-permute-done | bytes 524320 | tf_op jit(solution)/shard_map/while/body/eval_jaxpr/ppermute | solution.py:25
  188.5 5.2 collective-permute-start
  196.2 4.4 collective-permute-done.1
  203.1 9.8 %collective-permute-done.2 = bf16[1024,256]{1,0:T(8,128)(2,1)S(1)} collective-permute-done((bf16[1024,256]{1,0:T(8,128)(2,1)S(1)}, bf16[1024,256]{1,0:T(8,128)(2,1)S(1)}, u32[]{:S(2)}, u32[]{:S(2)}) %collective-permute-start.2) | collective-permute-done | bytes 524320 | tf_op jit(solution)/shard_map/while/body/eval_jaxpr/ppermute | solution.py:25
  212.9 5.2 collective-permute-start
  220.7 4.4 collective-permute-done.1
  227.5 9.8 %collective-permute-done.2 = bf16[1024,256]{1,0:T(8,128)(2,1)S(1)} collective-permute-done((bf16[1024,256]{1,0:T(8,128)(2,1)S(1)}, bf16[1024,256]{1,0:T(8,128)(2,1)S(1)}, u32[]{:S(2)}, u32[]{:S(2)}) %collective-permute-start.2) | collective-permute-done | bytes 524320 | tf_op jit(solution)/shard_map/while/body/eval_jaxpr/ppermute | solution.py:25
  237.4 5.2 collective-permute-start
  245.1 4.4 collective-permute-done.1
  252.0 9.8 %collective-permute-done.2 = bf16[1024,256]{1,0:T(8,128)(2,1)S(1)} collective-permute-done((bf16[1024,256]{1,0:T(8,128)(2,1)S(1)}, bf16[1024,256]{1,0:T(8,128)(2,1)S(1)}, u32[]{:S(2)}, u32[]{:S(2)}) %collective-permute-start.2) | collective-permute-done | bytes 524320 | tf_op jit(solution)/shard_map/while/body/eval_jaxpr/ppermute | solution.py:25
  261.8 5.2 collective-permute-start
  276.4 9.8 %collective-permute-done.2 = bf16[1024,256]{1,0:T(8,128)(2,1)S(1)} collective-permute-done((bf16[1024,256]{1,0:T(8,128)(2,1)S(1)}, bf16[1024,256]{1,0:T(8,128)(2,1)S(1)}, u32[]{:S(2)}, u32[]{:S(2)}) %collective-permute-start.2) | collective-permute-done | bytes 524320 | tf_op jit(solution)/shard_map/while/body/eval_jaxpr/ppermute | solution.py:25
  286.3 5.2 collective-permute-start
  300.9 9.8 %collective-permute-done.2 = bf16[1024,256]{1,0:T(8,128)(2,1)S(1)} collective-permute-done((bf16[1024,256]{1,0:T(8,128)(2,1)S(1)}, bf16[1024,256]{1,0:T(8,128)(2,1)S(1)}, u32[]{:S(2)}, u32[]{:S(2)}) %collective-permute-start.2) | collective-permute-done | bytes 524320 | tf_op jit(solution)/shard_map/while/body/eval_jaxpr/ppermute | solution.py:25
  310.7 5.2 collective-permute-start
  325.3 9.8 %collective-permute-done.2 = bf16[1024,256]{1,0:T(8,128)(2,1)S(1)} collective-permute-done((bf16[1024,256]{1,0:T(8,128)(2,1)S(1)}, bf16[1024,256]{1,0:T(8,128)(2,1)S(1)}, u32[]{:S(2)}, u32[]{:S(2)}) %collective-permute-start.2) | collective-permute-done | bytes 524320 | tf_op jit(solution)/shard_map/while/body/eval_jaxpr/ppermute | solution.py:25
  335.2 5.2 collective-permute-start
  349.8 9.8 %collective-permute-done.2 = bf16[1024,256]{1,0:T(8,128)(2,1)S(1)} collective-permute-done((bf16[1024,256]{1,0:T(8,128)(2,1)S(1)}, bf16[1024,256]{1,0:T(8,128)(2,1)S(1)}, u32[]{:S(2)}, u32[]{:S(2)}) %collective-permute-start.2) | collective-permute-done | bytes 524320 | tf_op jit(solution)/shard_map/while/body/eval_jaxpr/ppermute | solution.py:25
  359.6 5.2 collective-permute-start
  374.2 9.8 %collective-permute-done.2 = bf16[1024,256]{1,0:T(8,128)(2,1)S(1)} collective-permute-done((bf16[1024,256]{1,0:T(8,128)(2,1)S(1)}, bf16[1024,256]{1,0:T(8,128)(2,1)S(1)}, u32[]{:S(2)}, u32[]{:S(2)}) %collective-permute-start.2) | collective-permute-done | bytes 524320 | tf_op jit(solution)/shard_map/while/body/eval_jaxpr/ppermute | solution.py:25
  384.0 5.2 collective-permute-start
  398.7 9.8 %collective-permute-done.2 = bf16[1024,256]{1,0:T(8,128)(2,1)S(1)} collective-permute-done((bf16[1024,256]{1,0:T(8,128)(2,1)S(1)}, bf16[1024,256]{1,0:T(8,128)(2,1)S(1)}, u32[]{:S(2)}, u32[]{:S(2)}) %collective-permute-start.2) | collective-permute-done | bytes 524320 | tf_op jit(solution)/shard_map/while/body/eval_jaxpr/ppermute | solution.py:25
  409.5 151.6 %all-reduce.3.cloned.1.call-done = bf16[256,256]{0,1:T(8,128)(2,1)} async-done(((bf16[256,256]{0,1:T(8,128)(2,1)}), bf16[256,256]{0,1:T(8,128)(2,1)}) %all-reduce.3.cloned.1.call-update) | async-done | bytes 131088 | tf_op jit(solution)/shard_map/psum | solution.py:60
  563.2 11.7 %cholesky.50 = f32[128,128]{1,0:T(8,128)S(1)} custom-call(f32[128,128]{1,0:T(8,128)S(1)} %cholesky.118), custom_call_target="Cholesky" | custom-call | tf_op jit(solution)/shard_map/jit(cholesky)/cholesky | solution.py:63
  574.9 9.8 %custom-call.15 = f32[1,128,128]{1,2,0:T(8,128)S(1)} custom-call(f32[1,128,128]{2,1,0:T(8,128)S(1)} %get-tuple-element.62), custom_call_target="InvertDiagBlocksLowerTriangular" | custom-call | tf_op jit(solution)/shard_map/jit(cholesky)/cholesky | solution.py:63
  585.2 11.7 %cholesky.105 = f32[128,128]{1,0:T(8,128)S(1)} custom-call(f32[128,128]{1,0:T(8,128)S(1)} %convolution_subtract_fusion.1), custom_call_target="Cholesky" | custom-call | tf_op jit(solution)/shard_map/jit(cholesky)/cholesky | solution.py:63
  603.0 19.9 %custom-call.16 = f32[2,128,128]{1,2,0:T(8,128)S(1)} custom-call(f32[2,128,128]{2,1,0:T(8,128)S(1)} %get-tuple-element.32), custom_call_target="InvertDiagBlocksLowerTriangular" | custom-call | tf_op jit(solution)/shard_map/jit(_solve_triangular)/triangular_solve | solution.py:64
  (219 shorter events, 125.6 us)
Async XLA Ops:
  7.2 553.9 %all-reduce.3.cloned.1.call-start = ((), (), s32[]{:S(2)}) async-start(), calls=%async_computation | async-start | bytes 262144 | tf_op jit(solution)/shard_map/psum | solution.py:60
  10.4 10.3 %collective-permute-start = (bf16[256,256]{1,0:T(8,128)(2,1)S(1)}, bf16[256,256]{1,0:T(8,128)(2,1)S(1)}, u32[]{:S(2)}, u32[]{:S(2)}) collective-permute-start(bf16[256,256]{1,0:T(8,128)(2,1)S(1)} %get-tuple-element.117), channel_id=1, source_target_pairs={{1,0},{2,1},{3,2},{4,3},{5,4},{6,5},{7,6},{8,7},{9,8},{10,9},{11,1... | collective-permute-start | bytes 393224 | tf_op jit(solution)/shard_map/while/body/eval_jaxpr/ppermute | solution.py:17
  18.2 6.9 %collective-permute-start.1 = (bf16[256,256]{1,0:T(8,128)(2,1)S(1)}, bf16[256,256]{1,0:T(8,128)(2,1)S(1)}, u32[]{:S(2)}, u32[]{:S(2)}) collective-permute-start(bf16[256,256]{1,0:T(8,128)(2,1)S(1)} %get-tuple-element.118), channel_id=1, source_target_pairs={{0,1},{1,2},{2,3},{3,4},{4,5},{5,6},{6,7},{7,8},{8,9},{9,10},{10,1... | collective-permute-start | bytes 393224 | tf_op jit(solution)/shard_map/while/body/eval_jaxpr/ppermute | solution.py:16
  27.5 13.1 %collective-permute-start.2 = (bf16[1024,256]{1,0:T(8,128)(2,1)S(1)}, bf16[1024,256]{1,0:T(8,128)(2,1)S(1)}, u32[]{:S(2)}, u32[]{:S(2)}) collective-permute-start(bf16[1024,256]{1,0:T(8,128)(2,1)S(1)} %bitcast.85), channel_id=1, source_target_pairs={{0,32},{32,64},{64,96},{96,128},{128,160},{160,192},{192,224},{224... | collective-permute-start | bytes 1572872 | tf_op jit(solution)/shard_map/while/body/eval_jaxpr/ppermute | solution.py:25
  40.6 8.9 %collective-permute-start = (bf16[256,256]{1,0:T(8,128)(2,1)S(1)}, bf16[256,256]{1,0:T(8,128)(2,1)S(1)}, u32[]{:S(2)}, u32[]{:S(2)}) collective-permute-start(bf16[256,256]{1,0:T(8,128)(2,1)S(1)} %get-tuple-element.117), channel_id=1, source_target_pairs={{1,0},{2,1},{3,2},{4,3},{5,4},{6,5},{7,6},{8,7},{9,8},{10,9},{11,1... | collective-permute-start | bytes 393224 | tf_op jit(solution)/shard_map/while/body/eval_jaxpr/ppermute | solution.py:17
  47.0 6.9 %collective-permute-start.1 = (bf16[256,256]{1,0:T(8,128)(2,1)S(1)}, bf16[256,256]{1,0:T(8,128)(2,1)S(1)}, u32[]{:S(2)}, u32[]{:S(2)}) collective-permute-start(bf16[256,256]{1,0:T(8,128)(2,1)S(1)} %get-tuple-element.118), channel_id=1, source_target_pairs={{0,1},{1,2},{2,3},{3,4},{4,5},{5,6},{6,7},{7,8},{8,9},{9,10},{10,1... | collective-permute-start | bytes 393224 | tf_op jit(solution)/shard_map/while/body/eval_jaxpr/ppermute | solution.py:16
  56.4 9.8 %collective-permute-start.2 = (bf16[1024,256]{1,0:T(8,128)(2,1)S(1)}, bf16[1024,256]{1,0:T(8,128)(2,1)S(1)}, u32[]{:S(2)}, u32[]{:S(2)}) collective-permute-start(bf16[1024,256]{1,0:T(8,128)(2,1)S(1)} %bitcast.85), channel_id=1, source_target_pairs={{0,32},{32,64},{64,96},{96,128},{128,160},{160,192},{192,224},{224... | collective-permute-start | bytes 1572872 | tf_op jit(solution)/shard_map/while/body/eval_jaxpr/ppermute | solution.py:25
  66.2 7.8 %collective-permute-start = (bf16[256,256]{1,0:T(8,128)(2,1)S(1)}, bf16[256,256]{1,0:T(8,128)(2,1)S(1)}, u32[]{:S(2)}, u32[]{:S(2)}) collective-permute-start(bf16[256,256]{1,0:T(8,128)(2,1)S(1)} %get-tuple-element.117), channel_id=1, source_target_pairs={{1,0},{2,1},{3,2},{4,3},{5,4},{6,5},{7,6},{8,7},{9,8},{10,9},{11,1... | collective-permute-start | bytes 393224 | tf_op jit(solution)/shard_map/while/body/eval_jaxpr/ppermute | solution.py:17
  71.5 6.9 %collective-permute-start.1 = (bf16[256,256]{1,0:T(8,128)(2,1)S(1)}, bf16[256,256]{1,0:T(8,128)(2,1)S(1)}, u32[]{:S(2)}, u32[]{:S(2)}) collective-permute-start(bf16[256,256]{1,0:T(8,128)(2,1)S(1)} %get-tuple-element.118), channel_id=1, source_target_pairs={{0,1},{1,2},{2,3},{3,4},{4,5},{5,6},{6,7},{7,8},{8,9},{9,10},{10,1... | collective-permute-start | bytes 393224 | tf_op jit(solution)/shard_map/while/body/eval_jaxpr/ppermute | solution.py:16
  80.8 9.8 %collective-permute-start.2 = (bf16[1024,256]{1,0:T(8,128)(2,1)S(1)}, bf16[1024,256]{1,0:T(8,128)(2,1)S(1)}, u32[]{:S(2)}, u32[]{:S(2)}) collective-permute-start(bf16[1024,256]{1,0:T(8,128)(2,1)S(1)} %bitcast.85), channel_id=1, source_target_pairs={{0,32},{32,64},{64,96},{96,128},{128,160},{160,192},{192,224},{224... | collective-permute-start | bytes 1572872 | tf_op jit(solution)/shard_map/while/body/eval_jaxpr/ppermute | solution.py:25
  90.7 7.7 %collective-permute-start = (bf16[256,256]{1,0:T(8,128)(2,1)S(1)}, bf16[256,256]{1,0:T(8,128)(2,1)S(1)}, u32[]{:S(2)}, u32[]{:S(2)}) collective-permute-start(bf16[256,256]{1,0:T(8,128)(2,1)S(1)} %get-tuple-element.117), channel_id=1, source_target_pairs={{1,0},{2,1},{3,2},{4,3},{5,4},{6,5},{7,6},{8,7},{9,8},{10,9},{11,1... | collective-permute-start | bytes 393224 | tf_op jit(solution)/shard_map/while/body/eval_jaxpr/ppermute | solution.py:17
  95.9 6.9 %collective-permute-start.1 = (bf16[256,256]{1,0:T(8,128)(2,1)S(1)}, bf16[256,256]{1,0:T(8,128)(2,1)S(1)}, u32[]{:S(2)}, u32[]{:S(2)}) collective-permute-start(bf16[256,256]{1,0:T(8,128)(2,1)S(1)} %get-tuple-element.118), channel_id=1, source_target_pairs={{0,1},{1,2},{2,3},{3,4},{4,5},{5,6},{6,7},{7,8},{8,9},{9,10},{10,1... | collective-permute-start | bytes 393224 | tf_op jit(solution)/shard_map/while/body/eval_jaxpr/ppermute | solution.py:16
  105.3 9.8 %collective-permute-start.2 = (bf16[1024,256]{1,0:T(8,128)(2,1)S(1)}, bf16[1024,256]{1,0:T(8,128)(2,1)S(1)}, u32[]{:S(2)}, u32[]{:S(2)}) collective-permute-start(bf16[1024,256]{1,0:T(8,128)(2,1)S(1)} %bitcast.85), channel_id=1, source_target_pairs={{0,32},{32,64},{64,96},{96,128},{128,160},{160,192},{192,224},{224... | collective-permute-start | bytes 1572872 | tf_op jit(solution)/shard_map/while/body/eval_jaxpr/ppermute | solution.py:25
  115.1 7.8 %collective-permute-start = (bf16[256,256]{1,0:T(8,128)(2,1)S(1)}, bf16[256,256]{1,0:T(8,128)(2,1)S(1)}, u32[]{:S(2)}, u32[]{:S(2)}) collective-permute-start(bf16[256,256]{1,0:T(8,128)(2,1)S(1)} %get-tuple-element.117), channel_id=1, source_target_pairs={{1,0},{2,1},{3,2},{4,3},{5,4},{6,5},{7,6},{8,7},{9,8},{10,9},{11,1... | collective-permute-start | bytes 393224 | tf_op jit(solution)/shard_map/while/body/eval_jaxpr/ppermute | solution.py:17
  120.4 6.9 %collective-permute-start.1 = (bf16[256,256]{1,0:T(8,128)(2,1)S(1)}, bf16[256,256]{1,0:T(8,128)(2,1)S(1)}, u32[]{:S(2)}, u32[]{:S(2)}) collective-permute-start(bf16[256,256]{1,0:T(8,128)(2,1)S(1)} %get-tuple-element.118), channel_id=1, source_target_pairs={{0,1},{1,2},{2,3},{3,4},{4,5},{5,6},{6,7},{7,8},{8,9},{9,10},{10,1... | collective-permute-start | bytes 393224 | tf_op jit(solution)/shard_map/while/body/eval_jaxpr/ppermute | solution.py:16
  129.7 9.8 %collective-permute-start.2 = (bf16[1024,256]{1,0:T(8,128)(2,1)S(1)}, bf16[1024,256]{1,0:T(8,128)(2,1)S(1)}, u32[]{:S(2)}, u32[]{:S(2)}) collective-permute-start(bf16[1024,256]{1,0:T(8,128)(2,1)S(1)} %bitcast.85), channel_id=1, source_target_pairs={{0,32},{32,64},{64,96},{96,128},{128,160},{160,192},{192,224},{224... | collective-permute-start | bytes 1572872 | tf_op jit(solution)/shard_map/while/body/eval_jaxpr/ppermute | solution.py:25
  139.6 7.7 %collective-permute-start = (bf16[256,256]{1,0:T(8,128)(2,1)S(1)}, bf16[256,256]{1,0:T(8,128)(2,1)S(1)}, u32[]{:S(2)}, u32[]{:S(2)}) collective-permute-start(bf16[256,256]{1,0:T(8,128)(2,1)S(1)} %get-tuple-element.117), channel_id=1, source_target_pairs={{1,0},{2,1},{3,2},{4,3},{5,4},{6,5},{7,6},{8,7},{9,8},{10,9},{11,1... | collective-permute-start | bytes 393224 | tf_op jit(solution)/shard_map/while/body/eval_jaxpr/ppermute | solution.py:17
  144.8 6.9 %collective-permute-start.1 = (bf16[256,256]{1,0:T(8,128)(2,1)S(1)}, bf16[256,256]{1,0:T(8,128)(2,1)S(1)}, u32[]{:S(2)}, u32[]{:S(2)}) collective-permute-start(bf16[256,256]{1,0:T(8,128)(2,1)S(1)} %get-tuple-element.118), channel_id=1, source_target_pairs={{0,1},{1,2},{2,3},{3,4},{4,5},{5,6},{6,7},{7,8},{8,9},{9,10},{10,1... | collective-permute-start | bytes 393224 | tf_op jit(solution)/shard_map/while/body/eval_jaxpr/ppermute | solution.py:16
  154.2 9.8 %collective-permute-start.2 = (bf16[1024,256]{1,0:T(8,128)(2,1)S(1)}, bf16[1024,256]{1,0:T(8,128)(2,1)S(1)}, u32[]{:S(2)}, u32[]{:S(2)}) collective-permute-start(bf16[1024,256]{1,0:T(8,128)(2,1)S(1)} %bitcast.85), channel_id=1, source_target_pairs={{0,32},{32,64},{64,96},{96,128},{128,160},{160,192},{192,224},{224... | collective-permute-start | bytes 1572872 | tf_op jit(solution)/shard_map/while/body/eval_jaxpr/ppermute | solution.py:25
  164.0 7.8 %collective-permute-start = (bf16[256,256]{1,0:T(8,128)(2,1)S(1)}, bf16[256,256]{1,0:T(8,128)(2,1)S(1)}, u32[]{:S(2)}, u32[]{:S(2)}) collective-permute-start(bf16[256,256]{1,0:T(8,128)(2,1)S(1)} %get-tuple-element.117), channel_id=1, source_target_pairs={{1,0},{2,1},{3,2},{4,3},{5,4},{6,5},{7,6},{8,7},{9,8},{10,9},{11,1... | collective-permute-start | bytes 393224 | tf_op jit(solution)/shard_map/while/body/eval_jaxpr/ppermute | solution.py:17
  169.3 6.9 %collective-permute-start.1 = (bf16[256,256]{1,0:T(8,128)(2,1)S(1)}, bf16[256,256]{1,0:T(8,128)(2,1)S(1)}, u32[]{:S(2)}, u32[]{:S(2)}) collective-permute-start(bf16[256,256]{1,0:T(8,128)(2,1)S(1)} %get-tuple-element.118), channel_id=1, source_target_pairs={{0,1},{1,2},{2,3},{3,4},{4,5},{5,6},{6,7},{7,8},{8,9},{9,10},{10,1... | collective-permute-start | bytes 393224 | tf_op jit(solution)/shard_map/while/body/eval_jaxpr/ppermute | solution.py:16
  178.6 9.8 %collective-permute-start.2 = (bf16[1024,256]{1,0:T(8,128)(2,1)S(1)}, bf16[1024,256]{1,0:T(8,128)(2,1)S(1)}, u32[]{:S(2)}, u32[]{:S(2)}) collective-permute-start(bf16[1024,256]{1,0:T(8,128)(2,1)S(1)} %bitcast.85), channel_id=1, source_target_pairs={{0,32},{32,64},{64,96},{96,128},{128,160},{160,192},{192,224},{224... | collective-permute-start | bytes 1572872 | tf_op jit(solution)/shard_map/while/body/eval_jaxpr/ppermute | solution.py:25
  188.5 7.7 %collective-permute-start = (bf16[256,256]{1,0:T(8,128)(2,1)S(1)}, bf16[256,256]{1,0:T(8,128)(2,1)S(1)}, u32[]{:S(2)}, u32[]{:S(2)}) collective-permute-start(bf16[256,256]{1,0:T(8,128)(2,1)S(1)} %get-tuple-element.117), channel_id=1, source_target_pairs={{1,0},{2,1},{3,2},{4,3},{5,4},{6,5},{7,6},{8,7},{9,8},{10,9},{11,1... | collective-permute-start | bytes 393224 | tf_op jit(solution)/shard_map/while/body/eval_jaxpr/ppermute | solution.py:17
  193.7 6.9 %collective-permute-start.1 = (bf16[256,256]{1,0:T(8,128)(2,1)S(1)}, bf16[256,256]{1,0:T(8,128)(2,1)S(1)}, u32[]{:S(2)}, u32[]{:S(2)}) collective-permute-start(bf16[256,256]{1,0:T(8,128)(2,1)S(1)} %get-tuple-element.118), channel_id=1, source_target_pairs={{0,1},{1,2},{2,3},{3,4},{4,5},{5,6},{6,7},{7,8},{8,9},{9,10},{10,1... | collective-permute-start | bytes 393224 | tf_op jit(solution)/shard_map/while/body/eval_jaxpr/ppermute | solution.py:16
  203.1 9.8 %collective-permute-start.2 = (bf16[1024,256]{1,0:T(8,128)(2,1)S(1)}, bf16[1024,256]{1,0:T(8,128)(2,1)S(1)}, u32[]{:S(2)}, u32[]{:S(2)}) collective-permute-start(bf16[1024,256]{1,0:T(8,128)(2,1)S(1)} %bitcast.85), channel_id=1, source_target_pairs={{0,32},{32,64},{64,96},{96,128},{128,160},{160,192},{192,224},{224... | collective-permute-start | bytes 1572872 | tf_op jit(solution)/shard_map/while/body/eval_jaxpr/ppermute | solution.py:25
  212.9 7.8 %collective-permute-start = (bf16[256,256]{1,0:T(8,128)(2,1)S(1)}, bf16[256,256]{1,0:T(8,128)(2,1)S(1)}, u32[]{:S(2)}, u32[]{:S(2)}) collective-permute-start(bf16[256,256]{1,0:T(8,128)(2,1)S(1)} %get-tuple-element.117), channel_id=1, source_target_pairs={{1,0},{2,1},{3,2},{4,3},{5,4},{6,5},{7,6},{8,7},{9,8},{10,9},{11,1... | collective-permute-start | bytes 393224 | tf_op jit(solution)/shard_map/while/body/eval_jaxpr/ppermute | solution.py:17
  218.2 6.9 %collective-permute-start.1 = (bf16[256,256]{1,0:T(8,128)(2,1)S(1)}, bf16[256,256]{1,0:T(8,128)(2,1)S(1)}, u32[]{:S(2)}, u32[]{:S(2)}) collective-permute-start(bf16[256,256]{1,0:T(8,128)(2,1)S(1)} %get-tuple-element.118), channel_id=1, source_target_pairs={{0,1},{1,2},{2,3},{3,4},{4,5},{5,6},{6,7},{7,8},{8,9},{9,10},{10,1... | collective-permute-start | bytes 393224 | tf_op jit(solution)/shard_map/while/body/eval_jaxpr/ppermute | solution.py:16
  227.5 9.8 %collective-permute-start.2 = (bf16[1024,256]{1,0:T(8,128)(2,1)S(1)}, bf16[1024,256]{1,0:T(8,128)(2,1)S(1)}, u32[]{:S(2)}, u32[]{:S(2)}) collective-permute-start(bf16[1024,256]{1,0:T(8,128)(2,1)S(1)} %bitcast.85), channel_id=1, source_target_pairs={{0,32},{32,64},{64,96},{96,128},{128,160},{160,192},{192,224},{224... | collective-permute-start | bytes 1572872 | tf_op jit(solution)/shard_map/while/body/eval_jaxpr/ppermute | solution.py:25
  237.4 7.7 %collective-permute-start = (bf16[256,256]{1,0:T(8,128)(2,1)S(1)}, bf16[256,256]{1,0:T(8,128)(2,1)S(1)}, u32[]{:S(2)}, u32[]{:S(2)}) collective-permute-start(bf16[256,256]{1,0:T(8,128)(2,1)S(1)} %get-tuple-element.117), channel_id=1, source_target_pairs={{1,0},{2,1},{3,2},{4,3},{5,4},{6,5},{7,6},{8,7},{9,8},{10,9},{11,1... | collective-permute-start | bytes 393224 | tf_op jit(solution)/shard_map/while/body/eval_jaxpr/ppermute | solution.py:17
  242.6 6.9 %collective-permute-start.1 = (bf16[256,256]{1,0:T(8,128)(2,1)S(1)}, bf16[256,256]{1,0:T(8,128)(2,1)S(1)}, u32[]{:S(2)}, u32[]{:S(2)}) collective-permute-start(bf16[256,256]{1,0:T(8,128)(2,1)S(1)} %get-tuple-element.118), channel_id=1, source_target_pairs={{0,1},{1,2},{2,3},{3,4},{4,5},{5,6},{6,7},{7,8},{8,9},{9,10},{10,1... | collective-permute-start | bytes 393224 | tf_op jit(solution)/shard_map/while/body/eval_jaxpr/ppermute | solution.py:16
  252.0 9.8 %collective-permute-start.2 = (bf16[1024,256]{1,0:T(8,128)(2,1)S(1)}, bf16[1024,256]{1,0:T(8,128)(2,1)S(1)}, u32[]{:S(2)}, u32[]{:S(2)}) collective-permute-start(bf16[1024,256]{1,0:T(8,128)(2,1)S(1)} %bitcast.85), channel_id=1, source_target_pairs={{0,32},{32,64},{64,96},{96,128},{128,160},{160,192},{192,224},{224... | collective-permute-start | bytes 1572872 | tf_op jit(solution)/shard_map/while/body/eval_jaxpr/ppermute | solution.py:25
  261.8 7.8 %collective-permute-start = (bf16[256,256]{1,0:T(8,128)(2,1)S(1)}, bf16[256,256]{1,0:T(8,128)(2,1)S(1)}, u32[]{:S(2)}, u32[]{:S(2)}) collective-permute-start(bf16[256,256]{1,0:T(8,128)(2,1)S(1)} %get-tuple-element.117), channel_id=1, source_target_pairs={{1,0},{2,1},{3,2},{4,3},{5,4},{6,5},{7,6},{8,7},{9,8},{10,9},{11,1... | collective-permute-start | bytes 393224 | tf_op jit(solution)/shard_map/while/body/eval_jaxpr/ppermute | solution.py:17
  267.1 6.9 %collective-permute-start.1 = (bf16[256,256]{1,0:T(8,128)(2,1)S(1)}, bf16[256,256]{1,0:T(8,128)(2,1)S(1)}, u32[]{:S(2)}, u32[]{:S(2)}) collective-permute-start(bf16[256,256]{1,0:T(8,128)(2,1)S(1)} %get-tuple-element.118), channel_id=1, source_target_pairs={{0,1},{1,2},{2,3},{3,4},{4,5},{5,6},{6,7},{7,8},{8,9},{9,10},{10,1... | collective-permute-start | bytes 393224 | tf_op jit(solution)/shard_map/while/body/eval_jaxpr/ppermute | solution.py:16
  276.4 9.8 %collective-permute-start.2 = (bf16[1024,256]{1,0:T(8,128)(2,1)S(1)}, bf16[1024,256]{1,0:T(8,128)(2,1)S(1)}, u32[]{:S(2)}, u32[]{:S(2)}) collective-permute-start(bf16[1024,256]{1,0:T(8,128)(2,1)S(1)} %bitcast.85), channel_id=1, source_target_pairs={{0,32},{32,64},{64,96},{96,128},{128,160},{160,192},{192,224},{224... | collective-permute-start | bytes 1572872 | tf_op jit(solution)/shard_map/while/body/eval_jaxpr/ppermute | solution.py:25
  286.3 7.7 %collective-permute-start = (bf16[256,256]{1,0:T(8,128)(2,1)S(1)}, bf16[256,256]{1,0:T(8,128)(2,1)S(1)}, u32[]{:S(2)}, u32[]{:S(2)}) collective-permute-start(bf16[256,256]{1,0:T(8,128)(2,1)S(1)} %get-tuple-element.117), channel_id=1, source_target_pairs={{1,0},{2,1},{3,2},{4,3},{5,4},{6,5},{7,6},{8,7},{9,8},{10,9},{11,1... | collective-permute-start | bytes 393224 | tf_op jit(solution)/shard_map/while/body/eval_jaxpr/ppermute | solution.py:17
  291.5 6.9 %collective-permute-start.1 = (bf16[256,256]{1,0:T(8,128)(2,1)S(1)}, bf16[256,256]{1,0:T(8,128)(2,1)S(1)}, u32[]{:S(2)}, u32[]{:S(2)}) collective-permute-start(bf16[256,256]{1,0:T(8,128)(2,1)S(1)} %get-tuple-element.118), channel_id=1, source_target_pairs={{0,1},{1,2},{2,3},{3,4},{4,5},{5,6},{6,7},{7,8},{8,9},{9,10},{10,1... | collective-permute-start | bytes 393224 | tf_op jit(solution)/shard_map/while/body/eval_jaxpr/ppermute | solution.py:16
  300.9 9.8 %collective-permute-start.2 = (bf16[1024,256]{1,0:T(8,128)(2,1)S(1)}, bf16[1024,256]{1,0:T(8,128)(2,1)S(1)}, u32[]{:S(2)}, u32[]{:S(2)}) collective-permute-start(bf16[1024,256]{1,0:T(8,128)(2,1)S(1)} %bitcast.85), channel_id=1, source_target_pairs={{0,32},{32,64},{64,96},{96,128},{128,160},{160,192},{192,224},{224... | collective-permute-start | bytes 1572872 | tf_op jit(solution)/shard_map/while/body/eval_jaxpr/ppermute | solution.py:25
  310.7 7.8 %collective-permute-start = (bf16[256,256]{1,0:T(8,128)(2,1)S(1)}, bf16[256,256]{1,0:T(8,128)(2,1)S(1)}, u32[]{:S(2)}, u32[]{:S(2)}) collective-permute-start(bf16[256,256]{1,0:T(8,128)(2,1)S(1)} %get-tuple-element.117), channel_id=1, source_target_pairs={{1,0},{2,1},{3,2},{4,3},{5,4},{6,5},{7,6},{8,7},{9,8},{10,9},{11,1... | collective-permute-start | bytes 393224 | tf_op jit(solution)/shard_map/while/body/eval_jaxpr/ppermute | solution.py:17
  316.0 6.9 %collective-permute-start.1 = (bf16[256,256]{1,0:T(8,128)(2,1)S(1)}, bf16[256,256]{1,0:T(8,128)(2,1)S(1)}, u32[]{:S(2)}, u32[]{:S(2)}) collective-permute-start(bf16[256,256]{1,0:T(8,128)(2,1)S(1)} %get-tuple-element.118), channel_id=1, source_target_pairs={{0,1},{1,2},{2,3},{3,4},{4,5},{5,6},{6,7},{7,8},{8,9},{9,10},{10,1... | collective-permute-start | bytes 393224 | tf_op jit(solution)/shard_map/while/body/eval_jaxpr/ppermute | solution.py:16
  325.3 9.8 %collective-permute-start.2 = (bf16[1024,256]{1,0:T(8,128)(2,1)S(1)}, bf16[1024,256]{1,0:T(8,128)(2,1)S(1)}, u32[]{:S(2)}, u32[]{:S(2)}) collective-permute-start(bf16[1024,256]{1,0:T(8,128)(2,1)S(1)} %bitcast.85), channel_id=1, source_target_pairs={{0,32},{32,64},{64,96},{96,128},{128,160},{160,192},{192,224},{224... | collective-permute-start | bytes 1572872 | tf_op jit(solution)/shard_map/while/body/eval_jaxpr/ppermute | solution.py:25
  335.2 7.7 %collective-permute-start = (bf16[256,256]{1,0:T(8,128)(2,1)S(1)}, bf16[256,256]{1,0:T(8,128)(2,1)S(1)}, u32[]{:S(2)}, u32[]{:S(2)}) collective-permute-start(bf16[256,256]{1,0:T(8,128)(2,1)S(1)} %get-tuple-element.117), channel_id=1, source_target_pairs={{1,0},{2,1},{3,2},{4,3},{5,4},{6,5},{7,6},{8,7},{9,8},{10,9},{11,1... | collective-permute-start | bytes 393224 | tf_op jit(solution)/shard_map/while/body/eval_jaxpr/ppermute | solution.py:17
  340.4 6.9 %collective-permute-start.1 = (bf16[256,256]{1,0:T(8,128)(2,1)S(1)}, bf16[256,256]{1,0:T(8,128)(2,1)S(1)}, u32[]{:S(2)}, u32[]{:S(2)}) collective-permute-start(bf16[256,256]{1,0:T(8,128)(2,1)S(1)} %get-tuple-element.118), channel_id=1, source_target_pairs={{0,1},{1,2},{2,3},{3,4},{4,5},{5,6},{6,7},{7,8},{8,9},{9,10},{10,1... | collective-permute-start | bytes 393224 | tf_op jit(solution)/shard_map/while/body/eval_jaxpr/ppermute | solution.py:16
  349.7 9.8 %collective-permute-start.2 = (bf16[1024,256]{1,0:T(8,128)(2,1)S(1)}, bf16[1024,256]{1,0:T(8,128)(2,1)S(1)}, u32[]{:S(2)}, u32[]{:S(2)}) collective-permute-start(bf16[1024,256]{1,0:T(8,128)(2,1)S(1)} %bitcast.85), channel_id=1, source_target_pairs={{0,32},{32,64},{64,96},{96,128},{128,160},{160,192},{192,224},{224... | collective-permute-start | bytes 1572872 | tf_op jit(solution)/shard_map/while/body/eval_jaxpr/ppermute | solution.py:25
  359.6 7.8 %collective-permute-start = (bf16[256,256]{1,0:T(8,128)(2,1)S(1)}, bf16[256,256]{1,0:T(8,128)(2,1)S(1)}, u32[]{:S(2)}, u32[]{:S(2)}) collective-permute-start(bf16[256,256]{1,0:T(8,128)(2,1)S(1)} %get-tuple-element.117), channel_id=1, source_target_pairs={{1,0},{2,1},{3,2},{4,3},{5,4},{6,5},{7,6},{8,7},{9,8},{10,9},{11,1... | collective-permute-start | bytes 393224 | tf_op jit(solution)/shard_map/while/body/eval_jaxpr/ppermute | solution.py:17
  364.9 6.9 %collective-permute-start.1 = (bf16[256,256]{1,0:T(8,128)(2,1)S(1)}, bf16[256,256]{1,0:T(8,128)(2,1)S(1)}, u32[]{:S(2)}, u32[]{:S(2)}) collective-permute-start(bf16[256,256]{1,0:T(8,128)(2,1)S(1)} %get-tuple-element.118), channel_id=1, source_target_pairs={{0,1},{1,2},{2,3},{3,4},{4,5},{5,6},{6,7},{7,8},{8,9},{9,10},{10,1... | collective-permute-start | bytes 393224 | tf_op jit(solution)/shard_map/while/body/eval_jaxpr/ppermute | solution.py:16
  374.2 9.8 %collective-permute-start.2 = (bf16[1024,256]{1,0:T(8,128)(2,1)S(1)}, bf16[1024,256]{1,0:T(8,128)(2,1)S(1)}, u32[]{:S(2)}, u32[]{:S(2)}) collective-permute-start(bf16[1024,256]{1,0:T(8,128)(2,1)S(1)} %bitcast.85), channel_id=1, source_target_pairs={{0,32},{32,64},{64,96},{96,128},{128,160},{160,192},{192,224},{224... | collective-permute-start | bytes 1572872 | tf_op jit(solution)/shard_map/while/body/eval_jaxpr/ppermute | solution.py:25
  384.0 7.7 %collective-permute-start = (bf16[256,256]{1,0:T(8,128)(2,1)S(1)}, bf16[256,256]{1,0:T(8,128)(2,1)S(1)}, u32[]{:S(2)}, u32[]{:S(2)}) collective-permute-start(bf16[256,256]{1,0:T(8,128)(2,1)S(1)} %get-tuple-element.117), channel_id=1, source_target_pairs={{1,0},{2,1},{3,2},{4,3},{5,4},{6,5},{7,6},{8,7},{9,8},{10,9},{11,1... | collective-permute-start | bytes 393224 | tf_op jit(solution)/shard_map/while/body/eval_jaxpr/ppermute | solution.py:17
  398.6 9.8 %collective-permute-start.2 = (bf16[1024,256]{1,0:T(8,128)(2,1)S(1)}, bf16[1024,256]{1,0:T(8,128)(2,1)S(1)}, u32[]{:S(2)}, u32[]{:S(2)}) collective-permute-start(bf16[1024,256]{1,0:T(8,128)(2,1)S(1)} %bitcast.85), channel_id=1, source_target_pairs={{0,32},{32,64},{64,96},{96,128},{128,160},{160,192},{192,224},{224... | collective-permute-start | bytes 1572872 | tf_op jit(solution)/shard_map/while/body/eval_jaxpr/ppermute | solution.py:25
  (3 other events, 13.2 us)
Sparse Core Ops, SparseCore 0:
  409.6 151.4 all-reduce.2
where the time goes:
time: 636 us; the launch traced here: 634 us
  waiting for transfers between devices  388 us (61%)
  starting transfers between devices  119 us (19%)
  other arithmetic  60 us (9%)
  matrix products  31.2 us (5%)
  local copies, waits for them, and re-layouts  20.1 us (3%)
  between operations  15.5 us (2%)
    ppermute x16, waiting for transfers between devices, passed_along(): return lax.ppermute(value, axis, pairs)  160 us
    psum x1, waiting for transfers between devices, body(): lax.psum(gram_term.astype(jnp.bfloat16), 'rows').astype(jnp.float32)  152 us
    ppermute x16, starting transfers between devices, with_halo(): after = lax.ppermute(leading, axis, down)  87.6 us
    ppermute x16, waiting for transfers between devices, with_halo(): before = lax.ppermute(last, axis, up)  69.8 us
    another operation x6, other arithmetic, body(): lower_factor = jnp.linalg.cholesky(gram_total)  34 us
    ppermute x16, starting transfers between devices, with_halo(): before = lax.ppermute(last, axis, up)  30.7 us
    dot_general x16, matrix products, advance(): jnp.einsum('ijab,ijbk->iak', kept_blocks, picked, preferred_element_type=...  27.7 us
    another operation x2, other arithmetic, body(): jax.scipy.linalg.solve_triangular(lower_factor, arrived.astype(jnp.float3...  19.9 us
  transfers between devices with their start and end apart: 49, of which 49 were waited for; matrix products, arithmetic and copies ran while one was open for 0% of the time, Pallas kernels for 0%

commit v1 on v0

--- a/solution.py
+++ b/solution.py
@@ -57,9 +57,9 @@
     gram_term = lax.dot_general(
         arrived, arrived, (((0,), (0,)), ((), ())), preferred_element_type=jnp.float32
     )
-    gram_total = lax.psum(gram_term.astype(jnp.bfloat16), "rows").astype(jnp.float32) / (
-        rows_here * owners
-    )
+    gram_total = jnp.sum(lax.all_gather(gram_term.astype(jnp.bfloat16), "rows"), axis=0).astype(
+        jnp.float32
+    ) / (rows_here * owners)
     lower_factor = jnp.linalg.cholesky(gram_total)
     basis_out = jax.scipy.linalg.solve_triangular(
         lower_factor, arrived.astype(jnp.float32).T, lower=True

time: 636 us -> 570 us (0.90)
  the two profiles are of different devices: /device:TPU:2 before, /device:TPU:8 now
where the time goes in v1:
time: 570 us; the launch traced here: 568 us
  waiting for transfers between devices  345 us (61%)
  starting transfers between devices  94.4 us (17%)
  other arithmetic  60.9 us (11%)
  matrix products  30.8 us (5%)
  local copies, waits for them, and re-layouts  20.4 us (4%)
  between operations  15.5 us (3%)
    ppermute x16, waiting for transfers between devices, passed_along(): return lax.ppermute(value, axis, pairs)  161 us
    all_gather x1, waiting for transfers between devices, body(): lax.all_gather(gram_term.astype(jnp.bfloat16), 'rows')  87.1 us
    ppermute x16, waiting for transfers between devices, with_halo(): before = lax.ppermute(last, axis, up)  83.8 us
    ppermute x16, starting transfers between devices, with_halo(): after = lax.ppermute(leading, axis, down)  50 us
    ppermute x16, starting transfers between devices, with_halo(): before = lax.ppermute(last, axis, up)  44.1 us
    another operation x6, other arithmetic, body(): lower_factor = jnp.linalg.cholesky(gram_total)  34 us
    dot_general x16, matrix products, advance(): jnp.einsum('ijab,ijbk->iak', kept_blocks, picked, preferred_element_type=...  27.7 us
    another operation x2, other arithmetic, body(): jax.scipy.linalg.solve_triangular(lower_factor, arrived.astype(jnp.float3...  19.9 us
  transfers between devices with their start and end apart: 49, of which 49 were waited for; matrix products, arithmetic and copies ran while one was open for 1% of the time, Pallas kernels for 0%

profile of v1, /device:TPU:8, one launch (start us, length us, event | category | flops | bytes accessed | tf_op | source)
XLA Modules:
  0.0 567.9 jit_solution(8218325077468425349)
XLA Ops:
  10.4 395.5 %while.11 = (s32[]{:T(128)}, bf16[1024,256]{1,0:T(8,128)(2,1)S(1)}, s32[8,4]{0,1:T(4,128)S(1)}, bf16[8,4,128,128]{3,2,1,0:T(8,128)(2,1)}, s32[]{:T(128)}) while((s32[]{:T(128)}, bf16[1024,256]{1,0:T(8,128)(2,1)S(1)}, s32[8,4]{0,1:T(4,128)S(1)}, bf16[8,4,128,128]{3,2,1,0:T(8,128)(2,1)}, s32[]{:T(128)}) %tuple.55), condition=%wide.region_1.2_spmd, body=%wide.region_0.1_spmd.sunk | while | flops 271058016 | bytes 13112501 | solution.py:56
  10.4 4.6 collective-permute-start
  17.7 6.2 %collective-permute-done.1 = bf16[256,256]{1,0:T(8,128)(2,1)S(1)} collective-permute-done((bf16[256,256]{1,0:T(8,128)(2,1)S(1)}, bf16[256,256]{1,0:T(8,128)(2,1)S(1)}, u32[]{:S(2)}, u32[]{:S(2)}) %collective-permute-start.1) | collective-permute-done | bytes 131104 | tf_op jit(solution)/shard_map/while/body/eval_jaxpr/ppermute | solution.py:16
  26.4 13.9 %collective-permute-done.2 = bf16[1024,256]{1,0:T(8,128)(2,1)S(1)} collective-permute-done((bf16[1024,256]{1,0:T(8,128)(2,1)S(1)}, bf16[1024,256]{1,0:T(8,128)(2,1)S(1)}, u32[]{:S(2)}, u32[]{:S(2)}) %collective-permute-start.2) | collective-permute-done | bytes 524320 | tf_op jit(solution)/shard_map/while/body/eval_jaxpr/ppermute | solution.py:25
  42.3 3.9 collective-permute-start.1
  47.2 4.0 collective-permute-done.1
  53.8 9.8 %collective-permute-done.2 = bf16[1024,256]{1,0:T(8,128)(2,1)S(1)} collective-permute-done((bf16[1024,256]{1,0:T(8,128)(2,1)S(1)}, bf16[1024,256]{1,0:T(8,128)(2,1)S(1)}, u32[]{:S(2)}, u32[]{:S(2)}) %collective-permute-start.2) | collective-permute-done | bytes 524320 | tf_op jit(solution)/shard_map/while/body/eval_jaxpr/ppermute | solution.py:25
  65.7 3.8 collective-permute-start.1
  70.5 4.5 collective-permute-done.1
  77.5 9.8 %collective-permute-done.2 = bf16[1024,256]{1,0:T(8,128)(2,1)S(1)} collective-permute-done((bf16[1024,256]{1,0:T(8,128)(2,1)S(1)}, bf16[1024,256]{1,0:T(8,128)(2,1)S(1)}, u32[]{:S(2)}, u32[]{:S(2)}) %collective-permute-start.2) | collective-permute-done | bytes 524320 | tf_op jit(solution)/shard_map/while/body/eval_jaxpr/ppermute | solution.py:25
  87.3 3.9 collective-permute-start
  94.2 6.0 %collective-permute-done.1 = bf16[256,256]{1,0:T(8,128)(2,1)S(1)} collective-permute-done((bf16[256,256]{1,0:T(8,128)(2,1)S(1)}, bf16[256,256]{1,0:T(8,128)(2,1)S(1)}, u32[]{:S(2)}, u32[]{:S(2)}) %collective-permute-start.1) | collective-permute-done | bytes 131104 | tf_op jit(solution)/shard_map/while/body/eval_jaxpr/ppermute | solution.py:16
  102.8 9.8 %collective-permute-done.2 = bf16[1024,256]{1,0:T(8,128)(2,1)S(1)} collective-permute-done((bf16[1024,256]{1,0:T(8,128)(2,1)S(1)}, bf16[1024,256]{1,0:T(8,128)(2,1)S(1)}, u32[]{:S(2)}, u32[]{:S(2)}) %collective-permute-start.2) | collective-permute-done | bytes 524320 | tf_op jit(solution)/shard_map/while/body/eval_jaxpr/ppermute | solution.py:25
  119.4 5.3 collective-permute-done.1
  127.2 9.8 %collective-permute-done.2 = bf16[1024,256]{1,0:T(8,128)(2,1)S(1)} collective-permute-done((bf16[1024,256]{1,0:T(8,128)(2,1)S(1)}, bf16[1024,256]{1,0:T(8,128)(2,1)S(1)}, u32[]{:S(2)}, u32[]{:S(2)}) %collective-permute-start.2) | collective-permute-done | bytes 524320 | tf_op jit(solution)/shard_map/while/body/eval_jaxpr/ppermute | solution.py:25
  143.9 5.2 collective-permute-done.1
  151.6 9.8 %collective-permute-done.2 = bf16[1024,256]{1,0:T(8,128)(2,1)S(1)} collective-permute-done((bf16[1024,256]{1,0:T(8,128)(2,1)S(1)}, bf16[1024,256]{1,0:T(8,128)(2,1)S(1)}, u32[]{:S(2)}, u32[]{:S(2)}) %collective-permute-start.2) | collective-permute-done | bytes 524320 | tf_op jit(solution)/shard_map/while/body/eval_jaxpr/ppermute | solution.py:25
  161.5 3.1 collective-permute-start
  168.3 5.3 collective-permute-done.1
  176.1 9.8 %collective-permute-done.2 = bf16[1024,256]{1,0:T(8,128)(2,1)S(1)} collective-permute-done((bf16[1024,256]{1,0:T(8,128)(2,1)S(1)}, bf16[1024,256]{1,0:T(8,128)(2,1)S(1)}, u32[]{:S(2)}, u32[]{:S(2)}) %collective-permute-start.2) | collective-permute-done | bytes 524320 | tf_op jit(solution)/shard_map/while/body/eval_jaxpr/ppermute | solution.py:25
  192.8 5.2 collective-permute-done.1
  200.5 9.8 %collective-permute-done.2 = bf16[1024,256]{1,0:T(8,128)(2,1)S(1)} collective-permute-done((bf16[1024,256]{1,0:T(8,128)(2,1)S(1)}, bf16[1024,256]{1,0:T(8,128)(2,1)S(1)}, u32[]{:S(2)}, u32[]{:S(2)}) %collective-permute-start.2) | collective-permute-done | bytes 524320 | tf_op jit(solution)/shard_map/while/body/eval_jaxpr/ppermute | solution.py:25
  210.4 3.1 collective-permute-start
  217.2 5.3 collective-permute-done.1
  225.0 9.8 %collective-permute-done.2 = bf16[1024,256]{1,0:T(8,128)(2,1)S(1)} collective-permute-done((bf16[1024,256]{1,0:T(8,128)(2,1)S(1)}, bf16[1024,256]{1,0:T(8,128)(2,1)S(1)}, u32[]{:S(2)}, u32[]{:S(2)}) %collective-permute-start.2) | collective-permute-done | bytes 524320 | tf_op jit(solution)/shard_map/while/body/eval_jaxpr/ppermute | solution.py:25
  241.7 5.2 collective-permute-done.1
  249.4 9.8 %collective-permute-done.2 = bf16[1024,256]{1,0:T(8,128)(2,1)S(1)} collective-permute-done((bf16[1024,256]{1,0:T(8,128)(2,1)S(1)}, bf16[1024,256]{1,0:T(8,128)(2,1)S(1)}, u32[]{:S(2)}, u32[]{:S(2)}) %collective-permute-start.2) | collective-permute-done | bytes 524320 | tf_op jit(solution)/shard_map/while/body/eval_jaxpr/ppermute | solution.py:25
  259.2 3.1 collective-permute-start
  266.1 5.3 collective-permute-done.1
  273.9 9.8 %collective-permute-done.2 = bf16[1024,256]{1,0:T(8,128)(2,1)S(1)} collective-permute-done((bf16[1024,256]{1,0:T(8,128)(2,1)S(1)}, bf16[1024,256]{1,0:T(8,128)(2,1)S(1)}, u32[]{:S(2)}, u32[]{:S(2)}) %collective-permute-start.2) | collective-permute-done | bytes 524320 | tf_op jit(solution)/shard_map/while/body/eval_jaxpr/ppermute | solution.py:25
  290.6 5.2 collective-permute-done.1
  298.3 9.8 %collective-permute-done.2 = bf16[1024,256]{1,0:T(8,128)(2,1)S(1)} collective-permute-done((bf16[1024,256]{1,0:T(8,128)(2,1)S(1)}, bf16[1024,256]{1,0:T(8,128)(2,1)S(1)}, u32[]{:S(2)}, u32[]{:S(2)}) %collective-permute-start.2) | collective-permute-done | bytes 524320 | tf_op jit(solution)/shard_map/while/body/eval_jaxpr/ppermute | solution.py:25
  308.1 3.1 collective-permute-start
  315.0 5.3 collective-permute-done.1
  322.8 9.8 %collective-permute-done.2 = bf16[1024,256]{1,0:T(8,128)(2,1)S(1)} collective-permute-done((bf16[1024,256]{1,0:T(8,128)(2,1)S(1)}, bf16[1024,256]{1,0:T(8,128)(2,1)S(1)}, u32[]{:S(2)}, u32[]{:S(2)}) %collective-permute-start.2) | collective-permute-done | bytes 524320 | tf_op jit(solution)/shard_map/while/body/eval_jaxpr/ppermute | solution.py:25
  339.5 5.2 collective-permute-done.1
  347.2 9.8 %collective-permute-done.2 = bf16[1024,256]{1,0:T(8,128)(2,1)S(1)} collective-permute-done((bf16[1024,256]{1,0:T(8,128)(2,1)S(1)}, bf16[1024,256]{1,0:T(8,128)(2,1)S(1)}, u32[]{:S(2)}, u32[]{:S(2)}) %collective-permute-start.2) | collective-permute-done | bytes 524320 | tf_op jit(solution)/shard_map/while/body/eval_jaxpr/ppermute | solution.py:25
  357.0 3.1 collective-permute-start
  363.9 5.3 collective-permute-done.1
  371.7 9.8 %collective-permute-done.2 = bf16[1024,256]{1,0:T(8,128)(2,1)S(1)} collective-permute-done((bf16[1024,256]{1,0:T(8,128)(2,1)S(1)}, bf16[1024,256]{1,0:T(8,128)(2,1)S(1)}, u32[]{:S(2)}, u32[]{:S(2)}) %collective-permute-start.2) | collective-permute-done | bytes 524320 | tf_op jit(solution)/shard_map/while/body/eval_jaxpr/ppermute | solution.py:25
  388.3 5.2 collective-permute-done.1
  396.1 9.8 %collective-permute-done.2 = bf16[1024,256]{1,0:T(8,128)(2,1)S(1)} collective-permute-done((bf16[1024,256]{1,0:T(8,128)(2,1)S(1)}, bf16[1024,256]{1,0:T(8,128)(2,1)S(1)}, u32[]{:S(2)}, u32[]{:S(2)}) %collective-permute-start.2) | collective-permute-done | bytes 524320 | tf_op jit(solution)/shard_map/while/body/eval_jaxpr/ppermute | solution.py:25
  407.2 87.1 %all-gather.3.cloned.1.call-done = bf16[8192,256]{1,0:T(8,128)(2,1)} async-done(((bf16[256,256]{1,0:T(8,128)(2,1)}), bf16[8192,256]{1,0:T(8,128)(2,1)}) %all-gather.3.cloned.1.call-update) | async-done | bytes 4194320 | tf_op jit(solution)/shard_map/all_gather | solution.py:60
  497.4 11.7 %cholesky.50 = f32[128,128]{1,0:T(8,128)S(1)} custom-call(f32[128,128]{1,0:T(8,128)S(1)} %cholesky.118), custom_call_target="Cholesky" | custom-call | tf_op jit(solution)/shard_map/jit(cholesky)/cholesky | solution.py:63
  509.1 9.8 %custom-call.15 = f32[1,128,128]{1,2,0:T(8,128)S(1)} custom-call(f32[1,128,128]{2,1,0:T(8,128)S(1)} %get-tuple-element.64), custom_call_target="InvertDiagBlocksLowerTriangular" | custom-call | tf_op jit(solution)/shard_map/jit(cholesky)/cholesky | solution.py:63
  519.4 11.7 %cholesky.105 = f32[128,128]{1,0:T(8,128)S(1)} custom-call(f32[128,128]{1,0:T(8,128)S(1)} %convolution_subtract_fusion.1), custom_call_target="Cholesky" | custom-call | tf_op jit(solution)/shard_map/jit(cholesky)/cholesky | solution.py:63
  533.2 4.0 while.12
  537.2 19.9 %custom-call.16 = f32[2,128,128]{1,2,0:T(8,128)S(1)} custom-call(f32[2,128,128]{2,1,0:T(8,128)S(1)} %get-tuple-element.32), custom_call_target="InvertDiagBlocksLowerTriangular" | custom-call | tf_op jit(solution)/shard_map/jit(_solve_triangular)/triangular_solve | solution.py:64
  (221 shorter events, 134.5 us)
Async XLA Ops:
  7.2 487.1 %all-gather.3.cloned.1.call-start = ((), (), s32[]{:S(2)}) async-start(), calls=%async_computation | async-start | bytes 4325376 | tf_op jit(solution)/shard_map/all_gather | solution.py:60
  10.4 7.3 %collective-permute-start = (bf16[256,256]{1,0:T(8,128)(2,1)S(1)}, bf16[256,256]{1,0:T(8,128)(2,1)S(1)}, u32[]{:S(2)}, u32[]{:S(2)}) collective-permute-start(bf16[256,256]{1,0:T(8,128)(2,1)S(1)} %get-tuple-element.119), channel_id=1, source_target_pairs={{1,0},{2,1},{3,2},{4,3},{5,4},{6,5},{7,6},{8,7},{9,8},{10,9},{11,1... | collective-permute-start | bytes 393224 | tf_op jit(solution)/shard_map/while/body/eval_jaxpr/ppermute | solution.py:17
  15.0 9.0 %collective-permute-start.1 = (bf16[256,256]{1,0:T(8,128)(2,1)S(1)}, bf16[256,256]{1,0:T(8,128)(2,1)S(1)}, u32[]{:S(2)}, u32[]{:S(2)}) collective-permute-start(bf16[256,256]{1,0:T(8,128)(2,1)S(1)} %get-tuple-element.120), channel_id=1, source_target_pairs={{0,1},{1,2},{2,3},{3,4},{4,5},{5,6},{6,7},{7,8},{8,9},{9,10},{10,1... | collective-permute-start | bytes 393224 | tf_op jit(solution)/shard_map/while/body/eval_jaxpr/ppermute | solution.py:16
  26.4 13.9 %collective-permute-start.2 = (bf16[1024,256]{1,0:T(8,128)(2,1)S(1)}, bf16[1024,256]{1,0:T(8,128)(2,1)S(1)}, u32[]{:S(2)}, u32[]{:S(2)}) collective-permute-start(bf16[1024,256]{1,0:T(8,128)(2,1)S(1)} %bitcast.84), channel_id=1, source_target_pairs={{0,32},{32,64},{64,96},{96,128},{128,160},{160,192},{192,224},{224... | collective-permute-start | bytes 1572872 | tf_op jit(solution)/shard_map/while/body/eval_jaxpr/ppermute | solution.py:25
  40.4 6.9 %collective-permute-start = (bf16[256,256]{1,0:T(8,128)(2,1)S(1)}, bf16[256,256]{1,0:T(8,128)(2,1)S(1)}, u32[]{:S(2)}, u32[]{:S(2)}) collective-permute-start(bf16[256,256]{1,0:T(8,128)(2,1)S(1)} %get-tuple-element.119), channel_id=1, source_target_pairs={{1,0},{2,1},{3,2},{4,3},{5,4},{6,5},{7,6},{8,7},{9,8},{10,9},{11,1... | collective-permute-start | bytes 393224 | tf_op jit(solution)/shard_map/while/body/eval_jaxpr/ppermute | solution.py:17
  42.3 9.0 %collective-permute-start.1 = (bf16[256,256]{1,0:T(8,128)(2,1)S(1)}, bf16[256,256]{1,0:T(8,128)(2,1)S(1)}, u32[]{:S(2)}, u32[]{:S(2)}) collective-permute-start(bf16[256,256]{1,0:T(8,128)(2,1)S(1)} %get-tuple-element.120), channel_id=1, source_target_pairs={{0,1},{1,2},{2,3},{3,4},{4,5},{5,6},{6,7},{7,8},{8,9},{9,10},{10,1... | collective-permute-start | bytes 393224 | tf_op jit(solution)/shard_map/while/body/eval_jaxpr/ppermute | solution.py:16
  53.8 9.8 %collective-permute-start.2 = (bf16[1024,256]{1,0:T(8,128)(2,1)S(1)}, bf16[1024,256]{1,0:T(8,128)(2,1)S(1)}, u32[]{:S(2)}, u32[]{:S(2)}) collective-permute-start(bf16[1024,256]{1,0:T(8,128)(2,1)S(1)} %bitcast.84), channel_id=1, source_target_pairs={{0,32},{32,64},{64,96},{96,128},{128,160},{160,192},{192,224},{224... | collective-permute-start | bytes 1572872 | tf_op jit(solution)/shard_map/while/body/eval_jaxpr/ppermute | solution.py:25
  63.6 6.9 %collective-permute-start = (bf16[256,256]{1,0:T(8,128)(2,1)S(1)}, bf16[256,256]{1,0:T(8,128)(2,1)S(1)}, u32[]{:S(2)}, u32[]{:S(2)}) collective-permute-start(bf16[256,256]{1,0:T(8,128)(2,1)S(1)} %get-tuple-element.119), channel_id=1, source_target_pairs={{1,0},{2,1},{3,2},{4,3},{5,4},{6,5},{7,6},{8,7},{9,8},{10,9},{11,1... | collective-permute-start | bytes 393224 | tf_op jit(solution)/shard_map/while/body/eval_jaxpr/ppermute | solution.py:17
  65.7 9.3 %collective-permute-start.1 = (bf16[256,256]{1,0:T(8,128)(2,1)S(1)}, bf16[256,256]{1,0:T(8,128)(2,1)S(1)}, u32[]{:S(2)}, u32[]{:S(2)}) collective-permute-start(bf16[256,256]{1,0:T(8,128)(2,1)S(1)} %get-tuple-element.120), channel_id=1, source_target_pairs={{0,1},{1,2},{2,3},{3,4},{4,5},{5,6},{6,7},{7,8},{8,9},{9,10},{10,1... | collective-permute-start | bytes 393224 | tf_op jit(solution)/shard_map/while/body/eval_jaxpr/ppermute | solution.py:16
  77.5 9.8 %collective-permute-start.2 = (bf16[1024,256]{1,0:T(8,128)(2,1)S(1)}, bf16[1024,256]{1,0:T(8,128)(2,1)S(1)}, u32[]{:S(2)}, u32[]{:S(2)}) collective-permute-start(bf16[1024,256]{1,0:T(8,128)(2,1)S(1)} %bitcast.84), channel_id=1, source_target_pairs={{0,32},{32,64},{64,96},{96,128},{128,160},{160,192},{192,224},{224... | collective-permute-start | bytes 1572872 | tf_op jit(solution)/shard_map/while/body/eval_jaxpr/ppermute | solution.py:25
  87.3 6.9 %collective-permute-start = (bf16[256,256]{1,0:T(8,128)(2,1)S(1)}, bf16[256,256]{1,0:T(8,128)(2,1)S(1)}, u32[]{:S(2)}, u32[]{:S(2)}) collective-permute-start(bf16[256,256]{1,0:T(8,128)(2,1)S(1)} %get-tuple-element.119), channel_id=1, source_target_pairs={{1,0},{2,1},{3,2},{4,3},{5,4},{6,5},{7,6},{8,7},{9,8},{10,9},{11,1... | collective-permute-start | bytes 393224 | tf_op jit(solution)/shard_map/while/body/eval_jaxpr/ppermute | solution.py:17
  91.3 9.0 %collective-permute-start.1 = (bf16[256,256]{1,0:T(8,128)(2,1)S(1)}, bf16[256,256]{1,0:T(8,128)(2,1)S(1)}, u32[]{:S(2)}, u32[]{:S(2)}) collective-permute-start(bf16[256,256]{1,0:T(8,128)(2,1)S(1)} %get-tuple-element.120), channel_id=1, source_target_pairs={{0,1},{1,2},{2,3},{3,4},{4,5},{5,6},{6,7},{7,8},{8,9},{9,10},{10,1... | collective-permute-start | bytes 393224 | tf_op jit(solution)/shard_map/while/body/eval_jaxpr/ppermute | solution.py:16
  102.7 9.8 %collective-permute-start.2 = (bf16[1024,256]{1,0:T(8,128)(2,1)S(1)}, bf16[1024,256]{1,0:T(8,128)(2,1)S(1)}, u32[]{:S(2)}, u32[]{:S(2)}) collective-permute-start(bf16[1024,256]{1,0:T(8,128)(2,1)S(1)} %bitcast.84), channel_id=1, source_target_pairs={{0,32},{32,64},{64,96},{96,128},{128,160},{160,192},{192,224},{224... | collective-permute-start | bytes 1572872 | tf_op jit(solution)/shard_map/while/body/eval_jaxpr/ppermute | solution.py:25
  112.6 6.9 %collective-permute-start = (bf16[256,256]{1,0:T(8,128)(2,1)S(1)}, bf16[256,256]{1,0:T(8,128)(2,1)S(1)}, u32[]{:S(2)}, u32[]{:S(2)}) collective-permute-start(bf16[256,256]{1,0:T(8,128)(2,1)S(1)} %get-tuple-element.119), channel_id=1, source_target_pairs={{1,0},{2,1},{3,2},{4,3},{5,4},{6,5},{7,6},{8,7},{9,8},{10,9},{11,1... | collective-permute-start | bytes 393224 | tf_op jit(solution)/shard_map/while/body/eval_jaxpr/ppermute | solution.py:17
  115.7 9.0 %collective-permute-start.1 = (bf16[256,256]{1,0:T(8,128)(2,1)S(1)}, bf16[256,256]{1,0:T(8,128)(2,1)S(1)}, u32[]{:S(2)}, u32[]{:S(2)}) collective-permute-start(bf16[256,256]{1,0:T(8,128)(2,1)S(1)} %get-tuple-element.120), channel_id=1, source_target_pairs={{0,1},{1,2},{2,3},{3,4},{4,5},{5,6},{6,7},{7,8},{8,9},{9,10},{10,1... | collective-permute-start | bytes 393224 | tf_op jit(solution)/shard_map/while/body/eval_jaxpr/ppermute | solution.py:16
  127.2 9.8 %collective-permute-start.2 = (bf16[1024,256]{1,0:T(8,128)(2,1)S(1)}, bf16[1024,256]{1,0:T(8,128)(2,1)S(1)}, u32[]{:S(2)}, u32[]{:S(2)}) collective-permute-start(bf16[1024,256]{1,0:T(8,128)(2,1)S(1)} %bitcast.84), channel_id=1, source_target_pairs={{0,32},{32,64},{64,96},{96,128},{128,160},{160,192},{192,224},{224... | collective-permute-start | bytes 1572872 | tf_op jit(solution)/shard_map/while/body/eval_jaxpr/ppermute | solution.py:25
  137.0 6.9 %collective-permute-start = (bf16[256,256]{1,0:T(8,128)(2,1)S(1)}, bf16[256,256]{1,0:T(8,128)(2,1)S(1)}, u32[]{:S(2)}, u32[]{:S(2)}) collective-permute-start(bf16[256,256]{1,0:T(8,128)(2,1)S(1)} %get-tuple-element.119), channel_id=1, source_target_pairs={{1,0},{2,1},{3,2},{4,3},{5,4},{6,5},{7,6},{8,7},{9,8},{10,9},{11,1... | collective-permute-start | bytes 393224 | tf_op jit(solution)/shard_map/while/body/eval_jaxpr/ppermute | solution.py:17
  140.2 9.0 %collective-permute-start.1 = (bf16[256,256]{1,0:T(8,128)(2,1)S(1)}, bf16[256,256]{1,0:T(8,128)(2,1)S(1)}, u32[]{:S(2)}, u32[]{:S(2)}) collective-permute-start(bf16[256,256]{1,0:T(8,128)(2,1)S(1)} %get-tuple-element.120), channel_id=1, source_target_pairs={{0,1},{1,2},{2,3},{3,4},{4,5},{5,6},{6,7},{7,8},{8,9},{9,10},{10,1... | collective-permute-start | bytes 393224 | tf_op jit(solution)/shard_map/while/body/eval_jaxpr/ppermute | solution.py:16
  151.6 9.8 %collective-permute-start.2 = (bf16[1024,256]{1,0:T(8,128)(2,1)S(1)}, bf16[1024,256]{1,0:T(8,128)(2,1)S(1)}, u32[]{:S(2)}, u32[]{:S(2)}) collective-permute-start(bf16[1024,256]{1,0:T(8,128)(2,1)S(1)} %bitcast.84), channel_id=1, source_target_pairs={{0,32},{32,64},{64,96},{96,128},{128,160},{160,192},{192,224},{224... | collective-permute-start | bytes 1572872 | tf_op jit(solution)/shard_map/while/body/eval_jaxpr/ppermute | solution.py:25
  161.5 6.9 %collective-permute-start = (bf16[256,256]{1,0:T(8,128)(2,1)S(1)}, bf16[256,256]{1,0:T(8,128)(2,1)S(1)}, u32[]{:S(2)}, u32[]{:S(2)}) collective-permute-start(bf16[256,256]{1,0:T(8,128)(2,1)S(1)} %get-tuple-element.119), channel_id=1, source_target_pairs={{1,0},{2,1},{3,2},{4,3},{5,4},{6,5},{7,6},{8,7},{9,8},{10,9},{11,1... | collective-permute-start | bytes 393224 | tf_op jit(solution)/shard_map/while/body/eval_jaxpr/ppermute | solution.py:17
  164.6 9.0 %collective-permute-start.1 = (bf16[256,256]{1,0:T(8,128)(2,1)S(1)}, bf16[256,256]{1,0:T(8,128)(2,1)S(1)}, u32[]{:S(2)}, u32[]{:S(2)}) collective-permute-start(bf16[256,256]{1,0:T(8,128)(2,1)S(1)} %get-tuple-element.120), channel_id=1, source_target_pairs={{0,1},{1,2},{2,3},{3,4},{4,5},{5,6},{6,7},{7,8},{8,9},{9,10},{10,1... | collective-permute-start | bytes 393224 | tf_op jit(solution)/shard_map/while/body/eval_jaxpr/ppermute | solution.py:16
  176.1 9.8 %collective-permute-start.2 = (bf16[1024,256]{1,0:T(8,128)(2,1)S(1)}, bf16[1024,256]{1,0:T(8,128)(2,1)S(1)}, u32[]{:S(2)}, u32[]{:S(2)}) collective-permute-start(bf16[1024,256]{1,0:T(8,128)(2,1)S(1)} %bitcast.84), channel_id=1, source_target_pairs={{0,32},{32,64},{64,96},{96,128},{128,160},{160,192},{192,224},{224... | collective-permute-start | bytes 1572872 | tf_op jit(solution)/shard_map/while/body/eval_jaxpr/ppermute | solution.py:25
  185.9 6.9 %collective-permute-start = (bf16[256,256]{1,0:T(8,128)(2,1)S(1)}, bf16[256,256]{1,0:T(8,128)(2,1)S(1)}, u32[]{:S(2)}, u32[]{:S(2)}) collective-permute-start(bf16[256,256]{1,0:T(8,128)(2,1)S(1)} %get-tuple-element.119), channel_id=1, source_target_pairs={{1,0},{2,1},{3,2},{4,3},{5,4},{6,5},{7,6},{8,7},{9,8},{10,9},{11,1... | collective-permute-start | bytes 393224 | tf_op jit(solution)/shard_map/while/body/eval_jaxpr/ppermute | solution.py:17
  189.0 9.0 %collective-permute-start.1 = (bf16[256,256]{1,0:T(8,128)(2,1)S(1)}, bf16[256,256]{1,0:T(8,128)(2,1)S(1)}, u32[]{:S(2)}, u32[]{:S(2)}) collective-permute-start(bf16[256,256]{1,0:T(8,128)(2,1)S(1)} %get-tuple-element.120), channel_id=1, source_target_pairs={{0,1},{1,2},{2,3},{3,4},{4,5},{5,6},{6,7},{7,8},{8,9},{9,10},{10,1... | collective-permute-start | bytes 393224 | tf_op jit(solution)/shard_map/while/body/eval_jaxpr/ppermute | solution.py:16
  200.5 9.8 %collective-permute-start.2 = (bf16[1024,256]{1,0:T(8,128)(2,1)S(1)}, bf16[1024,256]{1,0:T(8,128)(2,1)S(1)}, u32[]{:S(2)}, u32[]{:S(2)}) collective-permute-start(bf16[1024,256]{1,0:T(8,128)(2,1)S(1)} %bitcast.84), channel_id=1, source_target_pairs={{0,32},{32,64},{64,96},{96,128},{128,160},{160,192},{192,224},{224... | collective-permute-start | bytes 1572872 | tf_op jit(solution)/shard_map/while/body/eval_jaxpr/ppermute | solution.py:25
  210.4 6.9 %collective-permute-start = (bf16[256,256]{1,0:T(8,128)(2,1)S(1)}, bf16[256,256]{1,0:T(8,128)(2,1)S(1)}, u32[]{:S(2)}, u32[]{:S(2)}) collective-permute-start(bf16[256,256]{1,0:T(8,128)(2,1)S(1)} %get-tuple-element.119), channel_id=1, source_target_pairs={{1,0},{2,1},{3,2},{4,3},{5,4},{6,5},{7,6},{8,7},{9,8},{10,9},{11,1... | collective-permute-start | bytes 393224 | tf_op jit(solution)/shard_map/while/body/eval_jaxpr/ppermute | solution.py:17
  213.5 9.0 %collective-permute-start.1 = (bf16[256,256]{1,0:T(8,128)(2,1)S(1)}, bf16[256,256]{1,0:T(8,128)(2,1)S(1)}, u32[]{:S(2)}, u32[]{:S(2)}) collective-permute-start(bf16[256,256]{1,0:T(8,128)(2,1)S(1)} %get-tuple-element.120), channel_id=1, source_target_pairs={{0,1},{1,2},{2,3},{3,4},{4,5},{5,6},{6,7},{7,8},{8,9},{9,10},{10,1... | collective-permute-start | bytes 393224 | tf_op jit(solution)/shard_map/while/body/eval_jaxpr/ppermute | solution.py:16
  225.0 9.8 %collective-permute-start.2 = (bf16[1024,256]{1,0:T(8,128)(2,1)S(1)}, bf16[1024,256]{1,0:T(8,128)(2,1)S(1)}, u32[]{:S(2)}, u32[]{:S(2)}) collective-permute-start(bf16[1024,256]{1,0:T(8,128)(2,1)S(1)} %bitcast.84), channel_id=1, source_target_pairs={{0,32},{32,64},{64,96},{96,128},{128,160},{160,192},{192,224},{224... | collective-permute-start | bytes 1572872 | tf_op jit(solution)/shard_map/while/body/eval_jaxpr/ppermute | solution.py:25
  234.8 6.9 %collective-permute-start = (bf16[256,256]{1,0:T(8,128)(2,1)S(1)}, bf16[256,256]{1,0:T(8,128)(2,1)S(1)}, u32[]{:S(2)}, u32[]{:S(2)}) collective-permute-start(bf16[256,256]{1,0:T(8,128)(2,1)S(1)} %get-tuple-element.119), channel_id=1, source_target_pairs={{1,0},{2,1},{3,2},{4,3},{5,4},{6,5},{7,6},{8,7},{9,8},{10,9},{11,1... | collective-permute-start | bytes 393224 | tf_op jit(solution)/shard_map/while/body/eval_jaxpr/ppermute | solution.py:17
  237.9 9.0 %collective-permute-start.1 = (bf16[256,256]{1,0:T(8,128)(2,1)S(1)}, bf16[256,256]{1,0:T(8,128)(2,1)S(1)}, u32[]{:S(2)}, u32[]{:S(2)}) collective-permute-start(bf16[256,256]{1,0:T(8,128)(2,1)S(1)} %get-tuple-element.120), channel_id=1, source_target_pairs={{0,1},{1,2},{2,3},{3,4},{4,5},{5,6},{6,7},{7,8},{8,9},{9,10},{10,1... | collective-permute-start | bytes 393224 | tf_op jit(solution)/shard_map/while/body/eval_jaxpr/ppermute | solution.py:16
  249.4 9.8 %collective-permute-start.2 = (bf16[1024,256]{1,0:T(8,128)(2,1)S(1)}, bf16[1024,256]{1,0:T(8,128)(2,1)S(1)}, u32[]{:S(2)}, u32[]{:S(2)}) collective-permute-start(bf16[1024,256]{1,0:T(8,128)(2,1)S(1)} %bitcast.84), channel_id=1, source_target_pairs={{0,32},{32,64},{64,96},{96,128},{128,160},{160,192},{192,224},{224... | collective-permute-start | bytes 1572872 | tf_op jit(solution)/shard_map/while/body/eval_jaxpr/ppermute | solution.py:25
  259.2 6.9 %collective-permute-start = (bf16[256,256]{1,0:T(8,128)(2,1)S(1)}, bf16[256,256]{1,0:T(8,128)(2,1)S(1)}, u32[]{:S(2)}, u32[]{:S(2)}) collective-permute-start(bf16[256,256]{1,0:T(8,128)(2,1)S(1)} %get-tuple-element.119), channel_id=1, source_target_pairs={{1,0},{2,1},{3,2},{4,3},{5,4},{6,5},{7,6},{8,7},{9,8},{10,9},{11,1... | collective-permute-start | bytes 393224 | tf_op jit(solution)/shard_map/while/body/eval_jaxpr/ppermute | solution.py:17
  262.4 9.0 %collective-permute-start.1 = (bf16[256,256]{1,0:T(8,128)(2,1)S(1)}, bf16[256,256]{1,0:T(8,128)(2,1)S(1)}, u32[]{:S(2)}, u32[]{:S(2)}) collective-permute-start(bf16[256,256]{1,0:T(8,128)(2,1)S(1)} %get-tuple-element.120), channel_id=1, source_target_pairs={{0,1},{1,2},{2,3},{3,4},{4,5},{5,6},{6,7},{7,8},{8,9},{9,10},{10,1... | collective-permute-start | bytes 393224 | tf_op jit(solution)/shard_map/while/body/eval_jaxpr/ppermute | solution.py:16
  273.8 9.8 %collective-permute-start.2 = (bf16[1024,256]{1,0:T(8,128)(2,1)S(1)}, bf16[1024,256]{1,0:T(8,128)(2,1)S(1)}, u32[]{:S(2)}, u32[]{:S(2)}) collective-permute-start(bf16[1024,256]{1,0:T(8,128)(2,1)S(1)} %bitcast.84), channel_id=1, source_target_pairs={{0,32},{32,64},{64,96},{96,128},{128,160},{160,192},{192,224},{224... | collective-permute-start | bytes 1572872 | tf_op jit(solution)/shard_map/while/body/eval_jaxpr/ppermute | solution.py:25
  283.7 6.9 %collective-permute-start = (bf16[256,256]{1,0:T(8,128)(2,1)S(1)}, bf16[256,256]{1,0:T(8,128)(2,1)S(1)}, u32[]{:S(2)}, u32[]{:S(2)}) collective-permute-start(bf16[256,256]{1,0:T(8,128)(2,1)S(1)} %get-tuple-element.119), channel_id=1, source_target_pairs={{1,0},{2,1},{3,2},{4,3},{5,4},{6,5},{7,6},{8,7},{9,8},{10,9},{11,1... | collective-permute-start | bytes 393224 | tf_op jit(solution)/shard_map/while/body/eval_jaxpr/ppermute | solution.py:17
  286.8 9.0 %collective-permute-start.1 = (bf16[256,256]{1,0:T(8,128)(2,1)S(1)}, bf16[256,256]{1,0:T(8,128)(2,1)S(1)}, u32[]{:S(2)}, u32[]{:S(2)}) collective-permute-start(bf16[256,256]{1,0:T(8,128)(2,1)S(1)} %get-tuple-element.120), channel_id=1, source_target_pairs={{0,1},{1,2},{2,3},{3,4},{4,5},{5,6},{6,7},{7,8},{8,9},{9,10},{10,1... | collective-permute-start | bytes 393224 | tf_op jit(solution)/shard_map/while/body/eval_jaxpr/ppermute | solution.py:16
  298.3 9.8 %collective-permute-start.2 = (bf16[1024,256]{1,0:T(8,128)(2,1)S(1)}, bf16[1024,256]{1,0:T(8,128)(2,1)S(1)}, u32[]{:S(2)}, u32[]{:S(2)}) collective-permute-start(bf16[1024,256]{1,0:T(8,128)(2,1)S(1)} %bitcast.84), channel_id=1, source_target_pairs={{0,32},{32,64},{64,96},{96,128},{128,160},{160,192},{192,224},{224... | collective-permute-start | bytes 1572872 | tf_op jit(solution)/shard_map/while/body/eval_jaxpr/ppermute | solution.py:25
  308.1 6.9 %collective-permute-start = (bf16[256,256]{1,0:T(8,128)(2,1)S(1)}, bf16[256,256]{1,0:T(8,128)(2,1)S(1)}, u32[]{:S(2)}, u32[]{:S(2)}) collective-permute-start(bf16[256,256]{1,0:T(8,128)(2,1)S(1)} %get-tuple-element.119), channel_id=1, source_target_pairs={{1,0},{2,1},{3,2},{4,3},{5,4},{6,5},{7,6},{8,7},{9,8},{10,9},{11,1... | collective-permute-start | bytes 393224 | tf_op jit(solution)/shard_map/while/body/eval_jaxpr/ppermute | solution.py:17
  311.3 9.0 %collective-permute-start.1 = (bf16[256,256]{1,0:T(8,128)(2,1)S(1)}, bf16[256,256]{1,0:T(8,128)(2,1)S(1)}, u32[]{:S(2)}, u32[]{:S(2)}) collective-permute-start(bf16[256,256]{1,0:T(8,128)(2,1)S(1)} %get-tuple-element.120), channel_id=1, source_target_pairs={{0,1},{1,2},{2,3},{3,4},{4,5},{5,6},{6,7},{7,8},{8,9},{9,10},{10,1... | collective-permute-start | bytes 393224 | tf_op jit(solution)/shard_map/while/body/eval_jaxpr/ppermute | solution.py:16
  322.7 9.8 %collective-permute-start.2 = (bf16[1024,256]{1,0:T(8,128)(2,1)S(1)}, bf16[1024,256]{1,0:T(8,128)(2,1)S(1)}, u32[]{:S(2)}, u32[]{:S(2)}) collective-permute-start(bf16[1024,256]{1,0:T(8,128)(2,1)S(1)} %bitcast.84), channel_id=1, source_target_pairs={{0,32},{32,64},{64,96},{96,128},{128,160},{160,192},{192,224},{224... | collective-permute-start | bytes 1572872 | tf_op jit(solution)/shard_map/while/body/eval_jaxpr/ppermute | solution.py:25
  332.6 6.9 %collective-permute-start = (bf16[256,256]{1,0:T(8,128)(2,1)S(1)}, bf16[256,256]{1,0:T(8,128)(2,1)S(1)}, u32[]{:S(2)}, u32[]{:S(2)}) collective-permute-start(bf16[256,256]{1,0:T(8,128)(2,1)S(1)} %get-tuple-element.119), channel_id=1, source_target_pairs={{1,0},{2,1},{3,2},{4,3},{5,4},{6,5},{7,6},{8,7},{9,8},{10,9},{11,1... | collective-permute-start | bytes 393224 | tf_op jit(solution)/shard_map/while/body/eval_jaxpr/ppermute | solution.py:17
  335.7 9.0 %collective-permute-start.1 = (bf16[256,256]{1,0:T(8,128)(2,1)S(1)}, bf16[256,256]{1,0:T(8,128)(2,1)S(1)}, u32[]{:S(2)}, u32[]{:S(2)}) collective-permute-start(bf16[256,256]{1,0:T(8,128)(2,1)S(1)} %get-tuple-element.120), channel_id=1, source_target_pairs={{0,1},{1,2},{2,3},{3,4},{4,5},{5,6},{6,7},{7,8},{8,9},{9,10},{10,1... | collective-permute-start | bytes 393224 | tf_op jit(solution)/shard_map/while/body/eval_jaxpr/ppermute | solution.py:16
  347.2 9.8 %collective-permute-start.2 = (bf16[1024,256]{1,0:T(8,128)(2,1)S(1)}, bf16[1024,256]{1,0:T(8,128)(2,1)S(1)}, u32[]{:S(2)}, u32[]{:S(2)}) collective-permute-start(bf16[1024,256]{1,0:T(8,128)(2,1)S(1)} %bitcast.84), channel_id=1, source_target_pairs={{0,32},{32,64},{64,96},{96,128},{128,160},{160,192},{192,224},{224... | collective-permute-start | bytes 1572872 | tf_op jit(solution)/shard_map/while/body/eval_jaxpr/ppermute | solution.py:25
  357.0 6.9 %collective-permute-start = (bf16[256,256]{1,0:T(8,128)(2,1)S(1)}, bf16[256,256]{1,0:T(8,128)(2,1)S(1)}, u32[]{:S(2)}, u32[]{:S(2)}) collective-permute-start(bf16[256,256]{1,0:T(8,128)(2,1)S(1)} %get-tuple-element.119), channel_id=1, source_target_pairs={{1,0},{2,1},{3,2},{4,3},{5,4},{6,5},{7,6},{8,7},{9,8},{10,9},{11,1... | collective-permute-start | bytes 393224 | tf_op jit(solution)/shard_map/while/body/eval_jaxpr/ppermute | solution.py:17
  360.2 9.0 %collective-permute-start.1 = (bf16[256,256]{1,0:T(8,128)(2,1)S(1)}, bf16[256,256]{1,0:T(8,128)(2,1)S(1)}, u32[]{:S(2)}, u32[]{:S(2)}) collective-permute-start(bf16[256,256]{1,0:T(8,128)(2,1)S(1)} %get-tuple-element.120), channel_id=1, source_target_pairs={{0,1},{1,2},{2,3},{3,4},{4,5},{5,6},{6,7},{7,8},{8,9},{9,10},{10,1... | collective-permute-start | bytes 393224 | tf_op jit(solution)/shard_map/while/body/eval_jaxpr/ppermute | solution.py:16
  371.6 9.8 %collective-permute-start.2 = (bf16[1024,256]{1,0:T(8,128)(2,1)S(1)}, bf16[1024,256]{1,0:T(8,128)(2,1)S(1)}, u32[]{:S(2)}, u32[]{:S(2)}) collective-permute-start(bf16[1024,256]{1,0:T(8,128)(2,1)S(1)} %bitcast.84), channel_id=1, source_target_pairs={{0,32},{32,64},{64,96},{96,128},{128,160},{160,192},{192,224},{224... | collective-permute-start | bytes 1572872 | tf_op jit(solution)/shard_map/while/body/eval_jaxpr/ppermute | solution.py:25
  384.6 9.0 %collective-permute-start.1 = (bf16[256,256]{1,0:T(8,128)(2,1)S(1)}, bf16[256,256]{1,0:T(8,128)(2,1)S(1)}, u32[]{:S(2)}, u32[]{:S(2)}) collective-permute-start(bf16[256,256]{1,0:T(8,128)(2,1)S(1)} %get-tuple-element.120), channel_id=1, source_target_pairs={{0,1},{1,2},{2,3},{3,4},{4,5},{5,6},{6,7},{7,8},{8,9},{9,10},{10,1... | collective-permute-start | bytes 393224 | tf_op jit(solution)/shard_map/while/body/eval_jaxpr/ppermute | solution.py:16
  396.1 9.8 %collective-permute-start.2 = (bf16[1024,256]{1,0:T(8,128)(2,1)S(1)}, bf16[1024,256]{1,0:T(8,128)(2,1)S(1)}, u32[]{:S(2)}, u32[]{:S(2)}) collective-permute-start(bf16[1024,256]{1,0:T(8,128)(2,1)S(1)} %bitcast.84), channel_id=1, source_target_pairs={{0,32},{32,64},{64,96},{96,128},{128,160},{160,192},{192,224},{224... | collective-permute-start | bytes 1572872 | tf_op jit(solution)/shard_map/while/body/eval_jaxpr/ppermute | solution.py:25
  (3 other events, 13.2 us)
Sparse Core Ops, SparseCore 0:
  407.1 87.1 all-gather.2
